TPU v7x, 128 devices: a whole 4x4x4 slice. The times are simulated.
128 devices in a mesh: req: 16 (over y_lo, z, core), tp: 8 (over y_hi, x).
Axes of the slice: x: 4, y: 4 (y_hi: 2, y_lo: 2; y = y_hi * 2 + y_lo), z: 4, core: 2. Of those that a mesh axis runs over, the one named last changes fastest.
Arguments:
- tokens: bfloat16 [2048, 2048], P('req')
- attn_gain: float32 [2048], replicated, may hold values from 0.25 to 1.75
- query_gain: float32 [128], replicated, may hold values from 0.8 to 2
- key_gain: float32 [128], replicated, may hold values from 0.8 to 2
- moe_gain: float32 [2048], replicated, may hold values from 0.25 to 1.75
- query_weight: float32 [2048, 2048], P('req', 'tp'), may hold values from -0.125 to 0.125
- key_weight: float32 [2048, 2048], P('req', 'tp'), may hold values from -0.125 to 0.125
- value_weight: float32 [2048, 2048], P('req', 'tp'), may hold values from -0.125 to 0.125
- out_weight: float32 [2048, 2048], P('tp', 'req'), may hold values from -0.125 to 0.125
- gate_weight: float32 [64, 2048, 1024], P(None, ('req', 'tp')), may hold values from -0.125 to 0.125
- up_weight: float32 [64, 2048, 1024], P(None, ('req', 'tp')), may hold values from -0.125 to 0.125
- down_weight: bfloat16 [128, 512, 2048], P(('req', 'tp')), may hold values from -0.1875 to 0.1875
- router_weight: bfloat16 [2048, 64], replicated, may hold values from -0.125 to 0.125
- page_store: bfloat16 [128, 128, 2, 2048], P('req', None, None, 'tp'), may hold values from -3 to 3
- prompt_lengths: int32 [32], replicated, may hold values from 32 to 96, as said below
- continues: int32 [32], replicated, may hold values from 0 to 1, as said below
- page_owner: int32 [16, 16], replicated, may hold values from 0 to 15, as said below
- page_slot: int32 [16, 16], replicated, may hold values from 0 to 7
- routes: int32 [2048, 8], P(('req', 'tp')), may hold values from 0 to 63, as said below
Outputs:
- server_qkv: bfloat16 [2048, 6144], P(None, 'tp')
- server_out: bfloat16 [2048, 2048], P('tp')
- server_gate_up: bfloat16 [128, 2048, 1024], P(('req', 'tp'))
- hidden: bfloat16 [2048, 2048], P(('req', 'tp'))
- new_cache: bfloat16 [2048, 2, 2048], P('req', None, 'tp')
Inputs may be any that keep to these rules, and one draw needn't show every extreme that they name: `prompt_lengths`: entries 2g and 2g + 1 are the two prompt lengths of group g and sum to 128. Exactly one of the two prompts of each group continues an earlier request. `page_owner`: no page of group g lies on g itself; at most 2 of a group's 16 pages lie on one owner, and every group has exactly 2 pages on some owner. `routes`: each row names 8 different experts. In each aligned block of 16 rows (the rows of one device) no expert is named by more than 3 rows, and one expert, the same in every block, is named by exactly 3 rows in each block.
All inputs are finite; a program needn't handle non-finite values.
Results may differ from a plain program's by a relative error of at most 0.0057.
Values may be sent and summed in bfloat16 or wider, within the bound.
A program may use at most 128 MiB of HBM per device.

v0:
```python
import math
import jax
import jax.numpy as jnp
from jax import lax
from jax.sharding import PartitionSpec as P

norm_eps = 1e-06
rope_base = 50000.0


def rms_scale(values, gain_vec):
    return (
        values * lax.rsqrt(jnp.mean(values * values, axis=-1, keepdims=True) + norm_eps) * gain_vec
    )


def rotate_half(values, cosine, sine_part):
    half_width = values.shape[-1] // 2
    first_half = values[..., :half_width]
    second_half = values[..., half_width:]
    return jnp.concatenate(
        [
            first_half * cosine - second_half * sine_part,
            second_half * cosine + first_half * sine_part,
        ],
        axis=-1,
    )


def split_halves(weights):
    expert_count, rows_here, hidden_units = weights.shape
    return weights.reshape(expert_count, rows_here, 2, hidden_units // 2).transpose(0, 2, 1, 3)


def body(
    tokens,
    attn_gain,
    query_gain,
    key_gain,
    moe_gain,
    query_weight,
    key_weight,
    value_weight,
    out_weight,
    gate_weight,
    up_weight,
    down_weight,
    router_weight,
    page_store,
    prompt_lengths,
    continues,
    page_owner,
    page_slot,
    routes,
):
    req_count = lax.axis_size("req")
    req_index = lax.axis_index("req")
    lane_index = lax.axis_index("tp")
    joined_local = jnp.concatenate(
        [
            query_weight.astype(jnp.bfloat16),
            key_weight.astype(jnp.bfloat16),
            value_weight.astype(jnp.bfloat16),
        ],
        axis=1,
    )
    server_qkv, server_out = (
        lax.all_gather(joined_local, "req", axis=0, tiled=True),
        lax.all_gather(out_weight.astype(jnp.bfloat16), "req", axis=1, tiled=True),
    )
    expert_count, rows_here, hidden_units = gate_weight.shape
    half_units = hidden_units // 2
    packed = jnp.concatenate(
        [
            split_halves(gate_weight.astype(jnp.bfloat16)),
            split_halves(up_weight.astype(jnp.bfloat16)),
        ],
        axis=3,
    ).reshape(2 * expert_count, rows_here, hidden_units)
    server_gate_up = lax.all_to_all(packed, ("req", "tp"), split_axis=0, concat_axis=1, tiled=True)
    group_rows, model_width = tokens.shape
    tokens_f32 = tokens.astype(jnp.float32)
    normed = rms_scale(tokens_f32, attn_gain).astype(jnp.bfloat16)
    projected = jnp.dot(normed, server_qkv, preferred_element_type=jnp.float32)
    head_dim = query_gain.shape[0]
    lane_width = server_qkv.shape[1] // 3
    lane_heads = lane_width // head_dim
    query_raw = projected[:, :lane_width].reshape(group_rows, lane_heads, head_dim)
    key_raw = projected[:, lane_width : 2 * lane_width].reshape(group_rows, lane_heads, head_dim)
    value_raw = projected[:, 2 * lane_width :]
    first_length = lax.dynamic_index_in_dim(prompt_lengths, 2 * req_index, 0, keepdims=False)
    carry_flags = lax.dynamic_slice_in_dim(continues, 2 * req_index, 2)
    row_ids = jnp.arange(group_rows, dtype=jnp.int32)
    second = (row_ids >= first_length).astype(jnp.int32)
    within = row_ids - second * first_length
    carried = jnp.where(second == 1, carry_flags[1], carry_flags[0])
    pages_per = page_owner.shape[1]
    page_rows = page_store.shape[1]
    context_len = pages_per * page_rows
    position = (within + context_len * carried).astype(jnp.float32)
    inverse = jnp.power(
        jnp.float32(rope_base), -(jnp.arange(head_dim // 2, dtype=jnp.float32) * 2.0 / head_dim)
    )
    angles = position[:, None, None] * inverse[None, None, :]
    cosine = jnp.cos(angles)
    sine_part = jnp.sin(angles)
    query_rows = rotate_half(rms_scale(query_raw, query_gain), cosine, sine_part).astype(
        jnp.bfloat16
    )
    keys_new = rotate_half(rms_scale(key_raw, key_gain), cosine, sine_part).astype(jnp.bfloat16)
    values_new = value_raw.astype(jnp.bfloat16)
    new_cache = jnp.stack([keys_new.reshape(group_rows, lane_width), values_new], axis=1)
    capacity = max(2, (pages_per + req_count - 2) // (req_count - 1))
    page_ids = jnp.arange(pages_per, dtype=jnp.int32)
    earlier = page_ids[None, :] < page_ids[:, None]
    same_owner = page_owner[:, :, None] == page_owner[:, None, :]
    page_rank = jnp.sum((same_owner & earlier[None]).astype(jnp.int32), axis=2)
    owned_here = page_owner == req_index
    chosen = owned_here[:, None, :] & (
        page_rank[:, None, :] == jnp.arange(capacity, dtype=jnp.int32)[None, :, None]
    )
    send_slot = jnp.sum(jnp.where(chosen, page_slot[:, None, :], 0), axis=2)
    send_live = jnp.any(chosen, axis=2)
    page_shape = page_store.shape[1:]
    outgoing_pages = jnp.take(page_store, send_slot.reshape(-1), axis=0).reshape(
        (req_count, capacity) + page_shape
    )
    outgoing_pages = jnp.where(
        send_live[:, :, None, None, None], outgoing_pages, jnp.zeros_like(outgoing_pages)
    )
    arrived_pages = lax.all_to_all(outgoing_pages, "req", split_axis=0, concat_axis=0, tiled=True)
    own_owner = jnp.take(page_owner, req_index, axis=0)
    own_rank = jnp.take(page_rank, req_index, axis=0)
    context = jnp.take(
        arrived_pages.reshape((req_count * capacity,) + page_shape),
        own_owner * capacity + own_rank,
        axis=0,
    )
    context = context.reshape(context_len, 2, lane_heads, head_dim)
    score_scale = 1.0 / math.sqrt(head_dim)
    near_scores = (
        jnp.einsum("ihc,jhc->hij", query_rows, keys_new, preferred_element_type=jnp.float32)
        * score_scale
    )
    far_scores = (
        jnp.einsum("ihc,jhc->hij", query_rows, context[:, 0], preferred_element_type=jnp.float32)
        * score_scale
    )
    same_request = second[:, None] == second[None, :]
    near_weights = jnp.where(same_request[None], jnp.exp(near_scores), jnp.float32(0.0))
    far_weights = jnp.where((carried == 1)[None, :, None], jnp.exp(far_scores), jnp.float32(0.0))
    totals = jnp.sum(near_weights, axis=2, keepdims=True) + jnp.sum(
        far_weights, axis=2, keepdims=True
    )
    near_probs = (near_weights / totals).astype(jnp.bfloat16)
    far_probs = (far_weights / totals).astype(jnp.bfloat16)
    attended = jnp.einsum(
        "hij,jhc->ihc",
        near_probs,
        values_new.reshape(group_rows, lane_heads, head_dim),
        preferred_element_type=jnp.float32,
    )
    attended = attended + jnp.einsum(
        "hij,jhc->ihc", far_probs, context[:, 1], preferred_element_type=jnp.float32
    )
    attended = attended.astype(jnp.bfloat16).reshape(group_rows, lane_width)
    shard_rows = routes.shape[0]
    row_start = lane_index * shard_rows
    head_terms = jnp.dot(attended, server_out, preferred_element_type=jnp.float32)
    mixed_all = lax.psum(head_terms, "tp")
    mixed_own = lax.dynamic_slice_in_dim(mixed_all, row_start, shard_rows, 0)
    residual_own = lax.dynamic_slice_in_dim(tokens_f32, row_start, shard_rows, 0) + mixed_own
    moe_own = rms_scale(residual_own, moe_gain).astype(jnp.bfloat16)
    logits = jnp.dot(moe_own, router_weight, preferred_element_type=jnp.float32)
    exps = jnp.exp(logits)
    routed_exps = jnp.take_along_axis(exps, routes, axis=1)
    entry_gates = routed_exps / jnp.sum(routed_exps, axis=1, keepdims=True)
    top_count = routes.shape[1]
    slot_depth = 3 * shard_rows * top_count // (2 * expert_count)
    flat_routes = routes.reshape(-1)
    onehot = (flat_routes[:, None] == jnp.arange(expert_count, dtype=jnp.int32)[None, :]).astype(
        jnp.int32
    )
    entry_rank = jnp.sum((jnp.cumsum(onehot, axis=0) - onehot) * onehot, axis=1)
    entry_slot = (flat_routes * slot_depth + entry_rank).reshape(shard_rows, top_count)
    select_table = jnp.any(
        entry_slot[None, :, :]
        == jnp.arange(expert_count * slot_depth, dtype=jnp.int32)[:, None, None],
        axis=2,
    ).astype(jnp.bfloat16)
    outgoing_rows = jnp.dot(select_table, moe_own, preferred_element_type=jnp.float32).astype(
        jnp.bfloat16
    )
    send_rows = jnp.broadcast_to(
        outgoing_rows.reshape(expert_count, 1, slot_depth, model_width),
        (expert_count, 2, slot_depth, model_width),
    ).reshape(2 * expert_count, slot_depth, model_width)
    arrived_rows = lax.all_to_all(send_rows, ("req", "tp"), split_axis=0, concat_axis=0, tiled=True)
    flat_rows = arrived_rows.reshape(-1, model_width)
    both = jnp.dot(flat_rows, server_gate_up[0], preferred_element_type=jnp.float32)
    act = (jax.nn.silu(both[:, :half_units]) * both[:, half_units:]).astype(jnp.bfloat16)
    expert_rows = (
        jnp.dot(act, down_weight[0], preferred_element_type=jnp.float32)
        .astype(jnp.bfloat16)
        .reshape(arrived_rows.shape)
    )
    returned = lax.all_to_all(expert_rows, ("req", "tp"), split_axis=0, concat_axis=0, tiled=True)
    returned = returned.reshape(expert_count, 2, slot_depth, model_width)
    joined_out = (returned[:, 0].astype(jnp.float32) + returned[:, 1].astype(jnp.float32)).reshape(
        expert_count * slot_depth, model_width
    )
    picked_rows = jnp.take(joined_out, entry_slot.reshape(-1), axis=0).reshape(
        shard_rows, top_count, model_width
    )
    moe_out = jnp.sum(picked_rows * entry_gates[:, :, None], axis=1)
    hidden_rows = (residual_own + moe_out).astype(jnp.bfloat16)
    return (server_qkv, server_out, server_gate_up, hidden_rows, new_cache)


def solution(mesh):
    in_specs = (
        P("req", None),
        P(),
        P(),
        P(),
        P(),
        P("req", "tp"),
        P("req", "tp"),
        P("req", "tp"),
        P("tp", "req"),
        P(None, ("req", "tp"), None),
        P(None, ("req", "tp"), None),
        P(("req", "tp"), None, None),
        P(),
        P("req", None, None, "tp"),
        P(),
        P(),
        P(),
        P(),
        P(("req", "tp"), None),
    )
    out_specs = (
        P(None, "tp"),
        P("tp", None),
        P(("req", "tp"), None, None),
        P(("req", "tp"), None),
        P("req", None, "tp"),
    )
    return jax.shard_map(body, mesh=mesh, in_specs=in_specs, out_specs=out_specs, check_vma=False)
```

profile of v0, /device:TPU:1, one launch (start us, length us, event | category | flops | bytes accessed | tf_op | source)
XLA Modules:
  0.0 396.9 jit_solution(3636944397927276136)
XLA Ops:
  14.1 10.0 %gather_fusion = bf16[32,128,2,256]{3,2,1,0:T(2,128)(2,1)} fusion(bf16[8,128,2,256]{3,2,1,0:T(2,128)(2,1)S(1)} %copy-done.1, s32[1024]{0:T(1024)S(1)} %pad_clamp_fusion.2), kind=kCustom, calls=%fused_computation | custom fusion | bytes 8388736 | tf_op jit(solution)/shard_map/jit(_take)/gather | solution.py:125
  24.2 4.2 %fusion = bf16[16,2,128,2,256]{4,2,3,1,0:T(8,128)(2,1)} fusion(bf16[16,2,128,2,256]{4,3,2,1,0:T(2,128)(2,1)} %bitcast.101, pred[16,2]{1,0:T(8,128)(4,1)S(1)} %copy.132, pred[16,2]{1,0:T(8,128)(4,1)S(1)} %copy.131), kind=kLoop, calls=%fused_computation.6 | loop fusion | flops 4194304 | bytes 8388672 | tf_op jit(solution)/shard_map/jit(_where)/select_n | solution.py:128
  28.4 8.1 %all-to-all-start.1 = ((bf16[16,2,128,2,256]{4,2,3,1,0:T(8,128)(2,1)}), bf16[16,2,128,2,256]{4,2,3,1,0:T(8,128)(2,1)}, u32[]{:S(2)}, u32[]{:S(2)}) async-start(bf16[16,2,128,2,256]{4,2,3,1,0:T(8,128)(2,1)} %fusion), calls=%async_computation.1 | async-start | bytes 8388608 | tf_op jit(solution)/shard_map/all_to_all | solution.py:131
  43.8 50.5 %all-to-all-done.1 = bf16[16,2,128,2,256]{4,2,3,1,0:T(8,128)(2,1)} async-done(((bf16[16,2,128,2,256]{4,2,3,1,0:T(8,128)(2,1)}), bf16[16,2,128,2,256]{4,2,3,1,0:T(8,128)(2,1)}, u32[]{:S(2)}, u32[]{:S(2)}) %all-to-all-start.1) | async-done | bytes 4194336 | tf_op jit(solution)/shard_map/all_to_all | solution.py:131
  94.4 4.2 %gather_fusion.1 = bf16[16,128,2,256]{3,1,2,0:T(8,128)(2,1)} fusion(bf16[32,128,2,256]{3,1,2,0:T(8,128)(2,1)} %bitcast.13, s32[1024]{0:T(1024)S(1)} %pad_clamp_fusion.1), kind=kCustom, calls=%fused_computation.1 | custom fusion | bytes 4194368 | tf_op jit(solution)/shard_map/jit(_take)/gather | solution.py:134
  98.6 4.5 %copy.135 = bf16[16,128,2,256]{1,0,3,2:T(8,128)(2,1)} copy(bf16[16,128,2,256]{3,1,2,0:T(8,128)(2,1)} %gather_fusion.1) | data formatting | bytes 4194304 | tf_op jit(solution)/shard_map/jit(_take)/gather | solution.py:134
  103.1 4.2 %gather.28 = bf16[2048,2,2,128]{0,3,2,1:T(8,128)(2,1)} reshape(bf16[16,128,2,256]{1,0,3,2:T(8,128)(2,1)} %copy.135) | data formatting | bytes 4194304 | tf_op jit(solution)/shard_map/jit(_take)/gather | solution.py:134
  107.3 4.0 copy.136
  126.0 81.6 %all-reduce.2.cloned.1.call-done = f32[128,2048]{1,0:T(8,128)} async-done(((f32[128,2048]{1,0:T(8,128)}), f32[128,2048]{1,0:T(8,128)}) %all-reduce.2.cloned.1.call-update) | async-done | bytes 1048592 | tf_op jit(solution)/shard_map/psum | solution.py:170
  215.0 11.8 %all-to-all-start.2 = ((bf16[128,3,2048]{2,1,0:T(4,128)(2,1)}), bf16[128,3,2048]{2,1,0:T(4,128)(2,1)}, u32[]{:S(2)}, u32[]{:S(2)}) async-start(bf16[128,3,2048]{2,1,0:T(4,128)(2,1)} %bitcast.102), calls=%async_computation.2 | async-start | bytes 4194304 | tf_op jit(solution)/shard_map/all_to_all | solution.py:198
  226.7 3.8 convert_element_type.113
  230.6 4.5 %reshape.372 = bf16[64,16,2,512]{3,2,1,0:T(2,128)(2,1)} reshape(bf16[64,16,1024]{2,1,0:T(8,128)(2,1)} %convert_element_type.113) | data formatting | bytes 4194304 | tf_op jit(solution)/shard_map/reshape | solution.py:32
  235.1 3.8 convert_element_type.114
  238.9 4.5 %reshape.373 = bf16[64,16,2,512]{3,2,1,0:T(2,128)(2,1)} reshape(bf16[64,16,1024]{2,1,0:T(8,128)(2,1)} %convert_element_type.114) | data formatting | bytes 4194304 | tf_op jit(solution)/shard_map/reshape | solution.py:32
  243.4 10.6 %pad_maximum_fusion = bf16[64,2,16,1024]{3,1,2,0:T(2,128)(2,1)} fusion(bf16[64,2,16,512]{3,1,2,0:T(2,128)(2,1)} %bitcast.104, bf16[64,2,16,512]{3,1,2,0:T(2,128)(2,1)} %bitcast.103), kind=kLoop, calls=%fused_computation.4 | loop fusion | flops 8388608 | bytes 8388608 | tf_op jit(solution)/shard_map/concatenate | solution.py:73
  254.0 5.6 %copy.126 = bf16[64,2,16,1024]{3,2,1,0:T(8,128)(2,1)} copy(bf16[64,2,16,1024]{3,1,2,0:T(2,128)(2,1)} %pad_maximum_fusion) | data formatting | bytes 8388608 | tf_op jit(solution)/shard_map/concatenate | solution.py:73
  259.6 10.2 %all-to-all-start = ((bf16[128,16,1024]{2,1,0:T(8,128)(2,1)}), bf16[128,16,1024]{2,1,0:T(8,128)(2,1)}, u32[]{:S(2)}, u32[]{:S(2)}) async-start(bf16[128,16,1024]{2,1,0:T(8,128)(2,1)} %bitcast.100), calls=%async_computation | async-start | bytes 8388608 | tf_op jit(solution)/shard_map/all_to_all | solution.py:80
  269.8 5.0 %reshape.383 = bf16[384,2048]{1,0:T(8,128)(2,1)} reshape(bf16[128,3,2048]{2,1,0:T(4,128)(2,1)} %all-to-all-done.2) | data formatting | bytes 3145728 | tf_op jit(solution)/shard_map/reshape | solution.py:199
  274.9 46.3 %all-to-all-done = bf16[128,16,1024]{2,1,0:T(8,128)(2,1)} async-done(((bf16[128,16,1024]{2,1,0:T(8,128)(2,1)}), bf16[128,16,1024]{2,1,0:T(8,128)(2,1)}, u32[]{:S(2)}, u32[]{:S(2)}) %all-to-all-start) | async-done | bytes 4194336 | tf_op jit(solution)/shard_map/all_to_all | solution.py:80
  321.1 4.4 %fusion.44 = f32[384,1024]{1,0:T(8,128)S(1)} fusion(bf16[384,2048]{1,0:T(8,128)(2,1)} %reshape.383, bf16[2048,1024]{1,0:T(8,128)(2,1)} %bitcast.19), kind=kOutput, calls=%fused_computation.128 | convolution fusion | flops 1610612736 | bytes 7340032 | tf_op jit(solution)/shard_map/dot_general | solution.py:200
  327.8 5.2 %reshape.384 = bf16[128,3,2048]{2,1,0:T(4,128)(2,1)} reshape(bf16[384,2048]{1,0:T(8,128)(2,1)} %convolution_convert_fusion) | data formatting | bytes 3145728 | tf_op jit(solution)/shard_map/reshape | solution.py:205
  332.9 7.4 %all-to-all-start.3 = ((bf16[128,3,2048]{2,1,0:T(4,128)(2,1)}), bf16[128,3,2048]{2,1,0:T(4,128)(2,1)}, u32[]{:S(2)}, u32[]{:S(2)}) async-start(bf16[128,3,2048]{2,1,0:T(4,128)(2,1)} %reshape.384), calls=%async_computation.3 | async-start | bytes 4194304 | tf_op jit(solution)/shard_map/all_to_all | solution.py:207
  344.5 24.4 %all-to-all-done.3 = bf16[128,3,2048]{2,1,0:T(4,128)(2,1)} async-done(((bf16[128,3,2048]{2,1,0:T(4,128)(2,1)}), bf16[128,3,2048]{2,1,0:T(4,128)(2,1)}, u32[]{:S(2)}, u32[]{:S(2)}) %all-to-all-start.3) | async-done | bytes 1572896 | tf_op jit(solution)/shard_map/all_to_all | solution.py:207
  385.7 4.6 %copy.170 = bf16[1,2048,1024]{2,1,0:T(8,128)(2,1)} copy(bf16[1,2048,1024]{2,1,0:T(8,128)(2,1)} %bitcast.3) | data formatting | bytes 8388608
  (137 shorter events, 59.2 us)
Async XLA Ops:
  7.2 318.4 %copy-start = (bf16[1,512,2048]{2,1,0:T(8,128)(2,1)S(1)}, bf16[1,512,2048]{2,1,0:T(8,128)(2,1)}, u32[]{:S(2)}) copy-start(bf16[1,512,2048]{2,1,0:T(8,128)(2,1)} %param.32) | copy-start | bytes 6291460
  7.2 7.0 %copy-start.1 = (bf16[8,128,2,256]{3,2,1,0:T(2,128)(2,1)S(1)}, bf16[8,128,2,256]{3,2,1,0:T(2,128)(2,1)}, u32[]{:S(2)}) copy-start(bf16[8,128,2,256]{3,2,1,0:T(2,128)(2,1)} %param.34) | copy-start | bytes 3145732
  7.2 106.8 %all-gather.3.cloned.1.call-start = ((), (), s32[]{:S(2)}) async-start(), calls=%async_computation.4 | async-start | bytes 3342336 | tf_op jit(solution)/shard_map/all_gather | solution.py:68
  28.4 8.1 %copy-start.8 = (f32[256,128]{1,0:T(8,128)S(1)}, f32[256,128]{1,0:T(8,128)}, u32[]{:S(2)}) copy-start(f32[256,128]{1,0:T(8,128)} %param.29) | copy-start | bytes 393220
  28.4 8.9 %copy-start.13 = (s32[32]{0:T(128)S(1)}, s32[32]{0:T(128)}, u32[]{:S(2)}) copy-start(s32[32]{0:T(128)} %param.36) | copy-start | bytes 388
  28.4 9.0 %copy-start.14 = (s32[32]{0:T(128)S(1)}, s32[32]{0:T(128)}, u32[]{:S(2)}) copy-start(s32[32]{0:T(128)} %param.35) | copy-start | bytes 388
  28.4 14.8 %copy-start.2 = (bf16[128,2048]{1,0:T(8,128)(2,1)S(1)}, bf16[128,2048]{1,0:T(8,128)(2,1)}, u32[]{:S(2)}) copy-start(bf16[128,2048]{1,0:T(8,128)(2,1)} %param.21) | copy-start | bytes 1572868
  28.4 66.0 %all-to-all-start.1 = ((bf16[16,2,128,2,256]{4,2,3,1,0:T(8,128)(2,1)}), bf16[16,2,128,2,256]{4,2,3,1,0:T(8,128)(2,1)}, u32[]{:S(2)}, u32[]{:S(2)}) async-start(bf16[16,2,128,2,256]{4,2,3,1,0:T(8,128)(2,1)} %fusion), calls=%async_computation.1 | async-start | bytes 8388608 | tf_op jit(solution)/shard_map/all_to_all | solution.py:131
  36.5 84.8 %all-gather.5.cloned.1.call-start = ((), (), s32[]{:S(2)}) async-start(), calls=%async_computation.5 | async-start | bytes 1114112 | tf_op jit(solution)/shard_map/all_gather | solution.py:69
  37.2 170.3 %all-reduce.2.cloned.1.call-start = ((), (), s32[]{:S(2)}) async-start(), calls=%async_computation.6 | async-start | bytes 2097152 | tf_op jit(solution)/shard_map/psum | solution.py:170
  111.2 2.8 copy-start.10
  114.0 4.2 %copy-start.11 = (f32[128]{0:T(128)S(1)}, f32[128]{0:T(128)}, u32[]{:S(2)}) copy-start(f32[128]{0:T(128)} %param.24) | copy-start | bytes 1540
  114.0 4.2 %copy-start.12 = (f32[128]{0:T(128)S(1)}, f32[128]{0:T(128)}, u32[]{:S(2)}) copy-start(f32[128]{0:T(128)} %param.23) | copy-start | bytes 1540
  116.5 0.8 copy-start.5
  118.2 1.6 copy-start.4
  121.3 3.6 copy-start.7
  123.9 84.8 %copy-start.9 = (f32[2048]{0:T(1024)S(1)}, f32[2048]{0:T(1024)}, u32[]{:S(2)}) copy-start(f32[2048]{0:T(1024)} %param.25) | copy-start | bytes 24580
  215.0 44.6 %all-to-all-start.2 = ((bf16[128,3,2048]{2,1,0:T(4,128)(2,1)}), bf16[128,3,2048]{2,1,0:T(4,128)(2,1)}, u32[]{:S(2)}, u32[]{:S(2)}) async-start(bf16[128,3,2048]{2,1,0:T(4,128)(2,1)} %bitcast.102), calls=%async_computation.2 | async-start | bytes 4194304 | tf_op jit(solution)/shard_map/all_to_all | solution.py:198
  259.6 61.5 %all-to-all-start = ((bf16[128,16,1024]{2,1,0:T(8,128)(2,1)}), bf16[128,16,1024]{2,1,0:T(8,128)(2,1)}, u32[]{:S(2)}, u32[]{:S(2)}) async-start(bf16[128,16,1024]{2,1,0:T(8,128)(2,1)} %bitcast.100), calls=%async_computation | async-start | bytes 8388608 | tf_op jit(solution)/shard_map/all_to_all | solution.py:80
  332.9 9.8 %copy-start.6 = (bf16[2048,64]{0,1:T(8,128)(2,1)S(1)}, bf16[2048,64]{0,1:T(8,128)(2,1)}, u32[]{:S(2)}) copy-start(bf16[2048,64]{0,1:T(8,128)(2,1)} %param.33) | copy-start | bytes 786436
  332.9 36.0 %all-to-all-start.3 = ((bf16[128,3,2048]{2,1,0:T(4,128)(2,1)}), bf16[128,3,2048]{2,1,0:T(4,128)(2,1)}, u32[]{:S(2)}, u32[]{:S(2)}) async-start(bf16[128,3,2048]{2,1,0:T(4,128)(2,1)} %reshape.384), calls=%async_computation.3 | async-start | bytes 4194304 | tf_op jit(solution)/shard_map/all_to_all | solution.py:207
  380.9 3.8 copy-start.3
Sparse Core Ops, SparseCore 0:
  11.0 65.5 all-gather.2
  78.7 38.0 all-gather.4
  124.0 83.4 all-reduce.1
where the time goes:
time: 399 us; the launch traced here: 397 us
  waiting for transfers between devices  203 us (51%)
  local copies, waits for them, and re-layouts  80.7 us (20%)
  other arithmetic  46.5 us (12%)
  starting transfers between devices  37.6 us (9%)
  matrix products  15 us (4%)
  between operations  14.2 us (4%)
    psum x1, waiting for transfers between devices, body(): mixed_all = lax.psum(head_terms, 'tp')  81.6 us
    all_to_all x1, waiting for transfers between devices, body(): lax.all_to_all(outgoing_pages, 'req', split_axis=0, concat_axis=0, tiled=...  50.5 us
    all_to_all x1, waiting for transfers between devices, body(): lax.all_to_all(packed, ('req', 'tp'), split_axis=0, concat_axis=1, tiled=...  46.3 us
    all_to_all x1, waiting for transfers between devices, body(): lax.all_to_all(expert_rows, ('req', 'tp'), split_axis=0, concat_axis=0, t...  24.4 us
    gather x4, local copies, waits for them, and re-layouts, body(): jnp.take(arrived_pages.reshape((req_count * capacity,) + page_shape), own...  16.8 us
    unnamed x35, local copies, waits for them, and re-layouts  11.9 us
    all_to_all x1, starting transfers between devices, body(): lax.all_to_all(send_rows, ('req', 'tp'), split_axis=0, concat_axis=0, til...  11.8 us
    concatenate x1, other arithmetic, body(): jnp.concatenate([split_halves(gate_weight.astype(jnp.bfloat16)), split_ha...  10.6 us
  transfers between devices with their start and end apart: 7, of which 4 were waited for; matrix products, arithmetic and copies ran while one was open for 24% of the time, Pallas kernels for 0%

commit v1 on v0

--- a/solution.py
+++ b/solution.py
@@ -167,7 +167,7 @@
     shard_rows = routes.shape[0]
     row_start = lane_index * shard_rows
     head_terms = jnp.dot(attended, server_out, preferred_element_type=jnp.float32)
-    mixed_all = lax.psum(head_terms, "tp")
+    mixed_all = jnp.sum(lax.all_gather(head_terms, "tp"), axis=0)
     mixed_own = lax.dynamic_slice_in_dim(mixed_all, row_start, shard_rows, 0)
     residual_own = lax.dynamic_slice_in_dim(tokens_f32, row_start, shard_rows, 0) + mixed_own
     moe_own = rms_scale(residual_own, moe_gain).astype(jnp.bfloat16)

time: 399 us -> 424 us (1.063)
  waiting for transfers between devices: 203 us -> 229 us
  starting transfers between devices: 37.6 us -> 32.9 us
    all_gather x0 -> x1, waiting for transfers between devices: none -> 107 us  [body(): mixed_all = jnp.sum(lax.all_gather(head_terms, 'tp'), axis=0)]
    psum x1 -> x0, waiting for transfers between devices: 81.6 us -> none  [body(): mixed_all = lax.psum(head_terms, 'tp')]
    all_to_all x1, starting transfers between devices: 11.8 us -> 7.08 us  [body(): lax.all_to_all(send_rows, ('req', 'tp'), split_axis=0, concat_axis=0, til...]
  transfers between devices with their start and end apart: 7 -> 7, of which waited for: 4 -> 4; matrix products, arithmetic and copies ran while one was open for 24% -> 22% of each run, Pallas kernels for 0% -> 0%
where the time goes in v1:
time: 424 us; the launch traced here: 422 us
  waiting for transfers between devices  229 us (54%)
  local copies, waits for them, and re-layouts  80.7 us (19%)
  other arithmetic  50.7 us (12%)
  starting transfers between devices  32.9 us (8%)
  matrix products  14.9 us (4%)
  between operations  14.2 us (3%)
    all_gather x1, waiting for transfers between devices, body(): mixed_all = jnp.sum(lax.all_gather(head_terms, 'tp'), axis=0)  107 us
    all_to_all x1, waiting for transfers between devices, body(): lax.all_to_all(outgoing_pages, 'req', split_axis=0, concat_axis=0, tiled=...  50.5 us
    all_to_all x1, waiting for transfers between devices, body(): lax.all_to_all(packed, ('req', 'tp'), split_axis=0, concat_axis=1, tiled=...  46.3 us
    all_to_all x1, waiting for transfers between devices, body(): lax.all_to_all(expert_rows, ('req', 'tp'), split_axis=0, concat_axis=0, t...  24.4 us
    gather x4, local copies, waits for them, and re-layouts, body(): jnp.take(arrived_pages.reshape((req_count * capacity,) + page_shape), own...  16.8 us
    unnamed x35, local copies, waits for them, and re-layouts  11.9 us
    concatenate x1, other arithmetic, body(): jnp.concatenate([split_halves(gate_weight.astype(jnp.bfloat16)), split_ha...  10.6 us
    all_to_all x1, starting transfers between devices, body(): lax.all_to_all(packed, ('req', 'tp'), split_axis=0, concat_axis=1, tiled=...  10.2 us
  transfers between devices with their start and end apart: 7, of which 4 were waited for; matrix products, arithmetic and copies ran while one was open for 22% of the time, Pallas kernels for 0%

profile of v1, /device:TPU:1, one launch (start us, length us, event | category | flops | bytes accessed | tf_op | source)
XLA Modules:
  0.0 422.1 jit_solution(14751181766524881702)
XLA Ops:
  14.1 10.0 %gather_fusion = bf16[32,128,2,256]{3,2,1,0:T(2,128)(2,1)} fusion(bf16[8,128,2,256]{3,2,1,0:T(2,128)(2,1)S(1)} %copy-done.1, s32[1024]{0:T(1024)S(1)} %pad_clamp_fusion.2), kind=kCustom, calls=%fused_computation | custom fusion | bytes 8388736 | tf_op jit(solution)/shard_map/jit(_take)/gather | solution.py:125
  24.2 4.2 fusion
  28.4 8.1 %all-to-all-start.1 = ((bf16[16,2,128,2,256]{4,2,3,1,0:T(8,128)(2,1)}), bf16[16,2,128,2,256]{4,2,3,1,0:T(8,128)(2,1)}, u32[]{:S(2)}, u32[]{:S(2)}) async-start(bf16[16,2,128,2,256]{4,2,3,1,0:T(8,128)(2,1)} %fusion), calls=%async_computation.1 | async-start | bytes 8388608 | tf_op jit(solution)/shard_map/all_to_all | solution.py:131
  43.8 50.5 %all-to-all-done.1 = bf16[16,2,128,2,256]{4,2,3,1,0:T(8,128)(2,1)} async-done(((bf16[16,2,128,2,256]{4,2,3,1,0:T(8,128)(2,1)}), bf16[16,2,128,2,256]{4,2,3,1,0:T(8,128)(2,1)}, u32[]{:S(2)}, u32[]{:S(2)}) %all-to-all-start.1) | async-done | bytes 4194336 | tf_op jit(solution)/shard_map/all_to_all | solution.py:131
  94.4 4.2 %gather_fusion.1 = bf16[16,128,2,256]{3,1,2,0:T(8,128)(2,1)} fusion(bf16[32,128,2,256]{3,1,2,0:T(8,128)(2,1)} %bitcast.13, s32[1024]{0:T(1024)S(1)} %pad_clamp_fusion.1), kind=kCustom, calls=%fused_computation.1 | custom fusion | bytes 4194368 | tf_op jit(solution)/shard_map/jit(_take)/gather | solution.py:134
  98.6 4.5 %copy.135 = bf16[16,128,2,256]{1,0,3,2:T(8,128)(2,1)} copy(bf16[16,128,2,256]{3,1,2,0:T(8,128)(2,1)} %gather_fusion.1) | data formatting | bytes 4194304 | tf_op jit(solution)/shard_map/jit(_take)/gather | solution.py:134
  103.1 4.2 gather.28
  107.3 4.0 copy.136
  126.0 107.3 %all-gather.9.cloned.1.call-done = f32[1024,2048]{1,0:T(8,128)} async-done(((f32[128,2048]{1,0:T(8,128)}), f32[1024,2048]{1,0:T(8,128)}) %all-gather.9.cloned.1.call-update) | async-done | bytes 8388624 | tf_op jit(solution)/shard_map/all_gather | solution.py:170
  233.3 4.2 reduce_sum.119
  244.9 7.1 %all-to-all-start.2 = ((bf16[128,3,2048]{2,1,0:T(4,128)(2,1)}), bf16[128,3,2048]{2,1,0:T(4,128)(2,1)}, u32[]{:S(2)}, u32[]{:S(2)}) async-start(bf16[128,3,2048]{2,1,0:T(4,128)(2,1)} %bitcast.104), calls=%async_computation.2 | async-start | bytes 4194304 | tf_op jit(solution)/shard_map/all_to_all | solution.py:198
  252.0 3.8 convert_element_type.113
  255.8 4.5 %reshape.372 = bf16[64,16,2,512]{3,2,1,0:T(2,128)(2,1)} reshape(bf16[64,16,1024]{2,1,0:T(8,128)(2,1)} %convert_element_type.113) | data formatting | bytes 4194304 | tf_op jit(solution)/shard_map/reshape | solution.py:32
  264.2 4.5 %reshape.373 = bf16[64,16,2,512]{3,2,1,0:T(2,128)(2,1)} reshape(bf16[64,16,1024]{2,1,0:T(8,128)(2,1)} %convert_element_type.114) | data formatting | bytes 4194304 | tf_op jit(solution)/shard_map/reshape | solution.py:32
  268.7 10.6 %pad_maximum_fusion = bf16[64,2,16,1024]{3,1,2,0:T(2,128)(2,1)} fusion(bf16[64,2,16,512]{3,1,2,0:T(2,128)(2,1)} %bitcast.106, bf16[64,2,16,512]{3,1,2,0:T(2,128)(2,1)} %bitcast.105), kind=kLoop, calls=%fused_computation.4 | loop fusion | flops 8388608 | bytes 8388608 | tf_op jit(solution)/shard_map/concatenate | solution.py:73
  279.2 5.6 %copy.126 = bf16[64,2,16,1024]{3,2,1,0:T(8,128)(2,1)} copy(bf16[64,2,16,1024]{3,1,2,0:T(2,128)(2,1)} %pad_maximum_fusion) | data formatting | bytes 8388608 | tf_op jit(solution)/shard_map/concatenate | solution.py:73
  284.8 10.2 %all-to-all-start = ((bf16[128,16,1024]{2,1,0:T(8,128)(2,1)}), bf16[128,16,1024]{2,1,0:T(8,128)(2,1)}, u32[]{:S(2)}, u32[]{:S(2)}) async-start(bf16[128,16,1024]{2,1,0:T(8,128)(2,1)} %bitcast.101), calls=%async_computation | async-start | bytes 8388608 | tf_op jit(solution)/shard_map/all_to_all | solution.py:80
  295.0 5.0 %reshape.383 = bf16[384,2048]{1,0:T(8,128)(2,1)} reshape(bf16[128,3,2048]{2,1,0:T(4,128)(2,1)} %all-to-all-done.2) | data formatting | bytes 3145728 | tf_op jit(solution)/shard_map/reshape | solution.py:199
  300.1 46.3 %all-to-all-done = bf16[128,16,1024]{2,1,0:T(8,128)(2,1)} async-done(((bf16[128,16,1024]{2,1,0:T(8,128)(2,1)}), bf16[128,16,1024]{2,1,0:T(8,128)(2,1)}, u32[]{:S(2)}, u32[]{:S(2)}) %all-to-all-start) | async-done | bytes 4194336 | tf_op jit(solution)/shard_map/all_to_all | solution.py:80
  346.4 4.4 %fusion.44 = f32[384,1024]{1,0:T(8,128)S(1)} fusion(bf16[384,2048]{1,0:T(8,128)(2,1)} %reshape.383, bf16[2048,1024]{1,0:T(8,128)(2,1)} %bitcast.20), kind=kOutput, calls=%fused_computation.128 | convolution fusion | flops 1610612736 | bytes 7340032 | tf_op jit(solution)/shard_map/dot_general | solution.py:200
  353.0 5.2 %reshape.384 = bf16[128,3,2048]{2,1,0:T(4,128)(2,1)} reshape(bf16[384,2048]{1,0:T(8,128)(2,1)} %convolution_convert_fusion) | data formatting | bytes 3145728 | tf_op jit(solution)/shard_map/reshape | solution.py:205
  358.2 7.5 %all-to-all-start.3 = ((bf16[128,3,2048]{2,1,0:T(4,128)(2,1)}), bf16[128,3,2048]{2,1,0:T(4,128)(2,1)}, u32[]{:S(2)}, u32[]{:S(2)}) async-start(bf16[128,3,2048]{2,1,0:T(4,128)(2,1)} %reshape.384), calls=%async_computation.3 | async-start | bytes 4194304 | tf_op jit(solution)/shard_map/all_to_all | solution.py:207
  369.7 24.4 %all-to-all-done.3 = bf16[128,3,2048]{2,1,0:T(4,128)(2,1)} async-done(((bf16[128,3,2048]{2,1,0:T(4,128)(2,1)}), bf16[128,3,2048]{2,1,0:T(4,128)(2,1)}, u32[]{:S(2)}, u32[]{:S(2)}) %all-to-all-start.3) | async-done | bytes 1572896 | tf_op jit(solution)/shard_map/all_to_all | solution.py:207
  410.9 4.6 %copy.169 = bf16[1,2048,1024]{2,1,0:T(8,128)(2,1)} copy(bf16[1,2048,1024]{2,1,0:T(8,128)(2,1)} %bitcast.3) | data formatting | bytes 8388608
  (138 shorter events, 63.0 us)
Async XLA Ops:
  7.2 343.7 %copy-start = (bf16[1,512,2048]{2,1,0:T(8,128)(2,1)S(1)}, bf16[1,512,2048]{2,1,0:T(8,128)(2,1)}, u32[]{:S(2)}) copy-start(bf16[1,512,2048]{2,1,0:T(8,128)(2,1)} %param.32) | copy-start | bytes 6291460
  7.2 7.0 %copy-start.1 = (bf16[8,128,2,256]{3,2,1,0:T(2,128)(2,1)S(1)}, bf16[8,128,2,256]{3,2,1,0:T(2,128)(2,1)}, u32[]{:S(2)}) copy-start(bf16[8,128,2,256]{3,2,1,0:T(2,128)(2,1)} %param.34) | copy-start | bytes 3145732
  7.2 106.8 %all-gather.5.cloned.1.call-start = ((), (), s32[]{:S(2)}) async-start(), calls=%async_computation.4 | async-start | bytes 3342336 | tf_op jit(solution)/shard_map/all_gather | solution.py:68
  28.4 8.1 %copy-start.8 = (f32[256,128]{1,0:T(8,128)S(1)}, f32[256,128]{1,0:T(8,128)}, u32[]{:S(2)}) copy-start(f32[256,128]{1,0:T(8,128)} %param.29) | copy-start | bytes 393220
  28.4 8.9 %copy-start.13 = (s32[32]{0:T(128)S(1)}, s32[32]{0:T(128)}, u32[]{:S(2)}) copy-start(s32[32]{0:T(128)} %param.36) | copy-start | bytes 388
  28.4 9.0 %copy-start.14 = (s32[32]{0:T(128)S(1)}, s32[32]{0:T(128)}, u32[]{:S(2)}) copy-start(s32[32]{0:T(128)} %param.35) | copy-start | bytes 388
  28.4 14.8 %copy-start.2 = (bf16[128,2048]{1,0:T(8,128)(2,1)S(1)}, bf16[128,2048]{1,0:T(8,128)(2,1)}, u32[]{:S(2)}) copy-start(bf16[128,2048]{1,0:T(8,128)(2,1)} %param.21) | copy-start | bytes 1572868
  28.4 66.0 %all-to-all-start.1 = ((bf16[16,2,128,2,256]{4,2,3,1,0:T(8,128)(2,1)}), bf16[16,2,128,2,256]{4,2,3,1,0:T(8,128)(2,1)}, u32[]{:S(2)}, u32[]{:S(2)}) async-start(bf16[16,2,128,2,256]{4,2,3,1,0:T(8,128)(2,1)} %fusion), calls=%async_computation.1 | async-start | bytes 8388608 | tf_op jit(solution)/shard_map/all_to_all | solution.py:131
  36.5 84.8 %all-gather.7.cloned.1.call-start = ((), (), s32[]{:S(2)}) async-start(), calls=%async_computation.5 | async-start | bytes 1114112 | tf_op jit(solution)/shard_map/all_gather | solution.py:69
  37.2 196.1 %all-gather.9.cloned.1.call-start = ((), (), s32[]{:S(2)}) async-start(), calls=%async_computation.6 | async-start | bytes 9437184 | tf_op jit(solution)/shard_map/all_gather | solution.py:170
  111.2 2.8 copy-start.10
  114.0 4.2 %copy-start.11 = (f32[128]{0:T(128)S(1)}, f32[128]{0:T(128)}, u32[]{:S(2)}) copy-start(f32[128]{0:T(128)} %param.24) | copy-start | bytes 1540
  114.0 4.2 %copy-start.12 = (f32[128]{0:T(128)S(1)}, f32[128]{0:T(128)}, u32[]{:S(2)}) copy-start(f32[128]{0:T(128)} %param.23) | copy-start | bytes 1540
  116.5 0.8 copy-start.5
  118.2 1.6 copy-start.4
  121.3 3.6 copy-start.7
  233.3 5.2 %copy-start.9 = (f32[2048]{0:T(1024)S(1)}, f32[2048]{0:T(1024)}, u32[]{:S(2)}) copy-start(f32[2048]{0:T(1024)} %param.25) | copy-start | bytes 24580
  244.9 39.9 %all-to-all-start.2 = ((bf16[128,3,2048]{2,1,0:T(4,128)(2,1)}), bf16[128,3,2048]{2,1,0:T(4,128)(2,1)}, u32[]{:S(2)}, u32[]{:S(2)}) async-start(bf16[128,3,2048]{2,1,0:T(4,128)(2,1)} %bitcast.104), calls=%async_computation.2 | async-start | bytes 4194304 | tf_op jit(solution)/shard_map/all_to_all | solution.py:198
  284.8 61.5 %all-to-all-start = ((bf16[128,16,1024]{2,1,0:T(8,128)(2,1)}), bf16[128,16,1024]{2,1,0:T(8,128)(2,1)}, u32[]{:S(2)}, u32[]{:S(2)}) async-start(bf16[128,16,1024]{2,1,0:T(8,128)(2,1)} %bitcast.101), calls=%async_computation | async-start | bytes 8388608 | tf_op jit(solution)/shard_map/all_to_all | solution.py:80
  358.2 9.8 %copy-start.6 = (bf16[2048,64]{0,1:T(8,128)(2,1)S(1)}, bf16[2048,64]{0,1:T(8,128)(2,1)}, u32[]{:S(2)}) copy-start(bf16[2048,64]{0,1:T(8,128)(2,1)} %param.33) | copy-start | bytes 786436
  358.2 36.0 %all-to-all-start.3 = ((bf16[128,3,2048]{2,1,0:T(4,128)(2,1)}), bf16[128,3,2048]{2,1,0:T(4,128)(2,1)}, u32[]{:S(2)}, u32[]{:S(2)}) async-start(bf16[128,3,2048]{2,1,0:T(4,128)(2,1)} %reshape.384), calls=%async_computation.3 | async-start | bytes 4194304 | tf_op jit(solution)/shard_map/all_to_all | solution.py:207
  406.1 3.8 copy-start.3
Sparse Core Ops, SparseCore 0:
  11.0 65.5 all-gather.4
  78.7 38.0 all-gather.6
  124.0 109.2 all-gather.8
